TPU v7x, 128 devices: a whole 4x4x4 slice. The times are simulated.
128 devices in a mesh: expert: 16 (over z, y), tensor: 8 (over x, core).
Axes of the slice: x: 4, y: 4, z: 4, core: 2. Of those that a mesh axis runs over, the one named last changes fastest.
Arguments:
- layer_input: bfloat16 [4096, 2, 4096], P('expert', None, 'tensor'), may hold values from -6 to 6
- base_input: bfloat16 [4096, 4096], P('expert', 'tensor'), may hold values from -6 to 6
- cotangent: bfloat16 [4096, 4096], P('expert', 'tensor'), may hold values from -6 to 6
- cross_weight: bfloat16 [16, 2, 4096, 4096], P('expert', None, 'tensor'), may hold values from -0.0625 to 0.0625
- cross_bias: float32 [16, 4096], P('expert', 'tensor'), may hold values from -3 to 3
- routes: int32 [4096, 2], P('expert'), may hold values from 0 to 15, as said below
- gate_values: float32 [4096, 2], P('expert'), may hold values from 0.2 to 1
Outputs:
- layer_out: bfloat16 [4096, 4096], P('expert', 'tensor')
- input_grad: bfloat16 [4096, 2, 4096], P('expert', None, 'tensor')
- base_grad: bfloat16 [4096, 4096], P('expert', 'tensor')
- weight_grad: bfloat16 [16, 2, 4096, 4096], P('expert', None, 'tensor')
- bias_grad: float32 [16, 4096], P('expert', 'tensor')
Inputs may be any that keep to these rules, and one draw needn't show every extreme that they name: `routes`: each row names two different experts. Among the 256 rows of one index of expert (aligned blocks), no expert is named more than 48 times, and one expert, the same in every block, is named exactly 48 times in every block.
All inputs are finite; a program needn't handle non-finite values.
Results may differ from a plain program's by a relative error of at most 0.017.
Values may be sent and summed in bfloat16 or wider, within the bound.
A program may use at most 128 MiB of HBM per device.

v0:
```python
import jax
import jax.numpy as jnp
from jax import lax
from jax.sharding import PartitionSpec as P


def route_positions(routes, experts, capacity):
    flat_routes = routes.reshape(-1)
    one_hot = (flat_routes[:, None] == jnp.arange(experts, dtype=jnp.int32)[None, :]).astype(
        jnp.int32
    )
    ranks = jnp.cumsum(one_hot, axis=0) - one_hot
    return flat_routes * capacity + jnp.sum(ranks * one_hot, axis=1)


def per_device(layer_input, base_input, cotangent, cross_weight, cross_bias, routes, gate_values):
    rows = layer_input.shape[0]
    width = layer_input.shape[2]
    full_out = cross_weight.shape[3]
    experts = lax.axis_size("expert")
    capacity = (3 * rows + experts - 1) // experts
    slots_total = experts * capacity
    scale = 1.0 / jnp.sqrt(jnp.float32(2 * rows))
    positions = route_positions(routes, experts, capacity)
    route_inputs = jnp.broadcast_to(layer_input[:, None], (rows, 2, 2, width)).reshape(
        2 * rows, 2, width
    )
    send_inputs = jnp.zeros((slots_total, 2, width), jnp.bfloat16).at[positions].set(route_inputs)
    send_inputs = send_inputs.reshape(experts, capacity, 2, width)
    weighted = (cotangent.astype(jnp.float32) * base_input.astype(jnp.float32)).astype(jnp.bfloat16)
    weighted_rows = lax.all_gather(weighted, "tensor", axis=1, tiled=True)
    cot_width = weighted_rows.shape[1]
    route_cot = (gate_values[:, :, None] * weighted_rows[:, None, :].astype(jnp.float32)).astype(
        jnp.bfloat16
    )
    send_cot = (
        jnp.zeros((slots_total, cot_width), jnp.bfloat16)
        .at[positions]
        .set(route_cot.reshape(2 * rows, cot_width))
    )
    send_cot = send_cot.reshape(experts, capacity, cot_width)
    arrived_inputs, arrived_cot = (
        lax.all_to_all(send_inputs, "expert", split_axis=0, concat_axis=0, tiled=True),
        lax.all_to_all(send_cot, "expert", split_axis=0, concat_axis=0, tiled=True),
    )
    flat_inputs = arrived_inputs.reshape(slots_total, 2 * width)
    flat_weight = cross_weight.reshape(2 * width, full_out)
    partial_value = jnp.dot(flat_inputs, flat_weight, preferred_element_type=jnp.float32)
    summed = lax.psum_scatter(
        partial_value.astype(jnp.bfloat16), "tensor", scatter_dimension=1, tiled=True
    ).astype(jnp.float32)
    cross = (summed + cross_bias).astype(jnp.bfloat16)
    returned = lax.all_to_all(
        cross.reshape(experts, capacity, width), "expert", split_axis=0, concat_axis=0, tiled=True
    )
    cross_routes = (
        returned.reshape(slots_total, width)[positions].reshape(rows, 2, width).astype(jnp.float32)
    )
    mixture = jnp.sum(gate_values[:, :, None] * cross_routes, axis=1)
    gate_total = jnp.sum(gate_values, axis=1)[:, None]
    layer_out = (
        base_input.astype(jnp.float32) * mixture
        + gate_total * layer_input[:, 0, :].astype(jnp.float32)
    ).astype(jnp.bfloat16)
    base_grad = (cotangent.astype(jnp.float32) * mixture).astype(jnp.bfloat16)
    cot_rows = arrived_cot.reshape(slots_total, cot_width)
    weight_sum = lax.dot_general(
        flat_inputs, cot_rows, (((0,), (0,)), ((), ())), preferred_element_type=jnp.float32
    )
    route_grads = lax.dot_general(
        cot_rows, flat_weight, (((1,), (1,)), ((), ())), preferred_element_type=jnp.float32
    )
    own_columns = lax.dynamic_slice_in_dim(cot_rows, lax.axis_index("tensor") * width, width, 1)
    bias_sum = jnp.sum(own_columns.astype(jnp.float32), axis=0)
    weight_grad = (weight_sum * scale).astype(jnp.bfloat16).reshape(1, 2, width, full_out)
    bias_grad = (bias_sum * scale).reshape(1, width)
    route_back = lax.all_to_all(
        route_grads.astype(jnp.bfloat16).reshape(experts, capacity, 2, width),
        "expert",
        split_axis=0,
        concat_axis=0,
        tiled=True,
    )
    picked = (
        route_back.reshape(slots_total, 2, width)[positions]
        .reshape(rows, 2, 2, width)
        .astype(jnp.float32)
    )
    grad_sum = jnp.sum(picked, axis=1)
    grad_sum = grad_sum.at[:, 0, :].add(gate_total * cotangent.astype(jnp.float32))
    input_grad = grad_sum.astype(jnp.bfloat16)
    return (layer_out, input_grad, base_grad, weight_grad, bias_grad)


def solution(mesh):
    in_specs = (
        P("expert", None, "tensor"),
        P("expert", "tensor"),
        P("expert", "tensor"),
        P("expert", None, "tensor", None),
        P("expert", "tensor"),
        P("expert", None),
        P("expert", None),
    )
    out_specs = (
        P("expert", "tensor"),
        P("expert", None, "tensor"),
        P("expert", "tensor"),
        P("expert", None, "tensor", None),
        P("expert", "tensor"),
    )
    return jax.shard_map(
        per_device, mesh=mesh, in_specs=in_specs, out_specs=out_specs, check_vma=False
    )
```

profile of v0, /device:TPU:0, one launch (start us, length us, event | category | flops | bytes accessed | tf_op | source)
XLA Modules:
  0.0 356.7 jit_solution(16559496350380601480)
XLA Ops:
  7.2 0.0 reduce-scatter.2.cloned.1.call-start
  7.2 0.7 broadcast_multiply_fusion.1
  7.9 0.8 copy.32
  8.7 0.1 eq.29
  8.9 0.1 eq.25
  9.0 0.1 copy.31
  9.1 0.1 mul.96
  9.3 1.2 reduce-window.6
  10.5 0.2 slice_reduce_fusion
  10.7 0.1 fusion.9
  10.8 1.6 broadcast_in_dim.7
  12.4 0.8 broadcast_in_dim.6
  13.2 13.8 %scatter_fusion = bf16[768,2,512]{2,1,0:T(2,128)(2,1)S(1)} fusion(bf16[768,2,512]{2,1,0:T(2,128)(2,1)S(1)} %broadcast_in_dim.6, s32[512]{0:T(512)S(1)} %bitcast.61, bf16[512,2,512]{2,1,0:T(2,128)(2,1)S(1)} %bitcast.57), kind=kCustom, calls=%fused_computation.2 | custom fusion | bytes 3147776 | tf_op jit(solution)/shard_map/scatter | solution.py:28
  27.1 30.7 %all_to_all.20 = bf16[16,48,2,512]{3,2,1,0:T(2,128)(2,1)S(1)} all-to-all(bf16[16,48,2,512]{3,2,1,0:T(2,128)(2,1)S(1)} %bitcast.54), channel_id=1, replica_groups=mesh['expert'=16,'tensor'=8] {'expert'}, dimensions={0} | all-to-all | bytes 3145728 | tf_op jit(solution)/shard_map/all_to_all | solution.py:43
  57.8 0.4 copy.39
  58.2 1.2 copy-done.1
  59.5 11.9 %convolution_convert_fusion = bf16[768,4096]{1,0:T(8,128)(2,1)} fusion(bf16[768,1024]{1,0:T(8,128)(2,1)S(1)} %bitcast.59, bf16[1024,4096]{1,0:T(8,128)(2,1)} %bitcast.67), kind=kOutput, calls=%fused_computation.6 | convolution fusion | flops 6445596672 | bytes 16252928 | tf_op jit(solution)/shard_map/dot_general | solution.py:48
  71.4 0.0 reduce-scatter.2.cloned.1.call-update
  71.4 40.0 %reduce-scatter.2.cloned.1.call-done = bf16[768,512]{1,0:T(8,128)(2,1)} async-done(((bf16[768,4096]{1,0:T(8,128)(2,1)}), bf16[768,512]{1,0:T(8,128)(2,1)}) %reduce-scatter.2.cloned.1.call-update) | async-done | bytes 786448 | tf_op jit(solution)/shard_map/reduce_scatter | solution.py:49
  111.5 2.2 add_convert_fusion
  113.6 7.0 %all-to-all-start.1 = ((bf16[16,48,512]{2,1,0:T(8,128)(2,1)}), bf16[16,48,512]{2,1,0:T(8,128)(2,1)S(1)}, u32[]{:S(2)}, u32[]{:S(2)}) async-start(bf16[16,48,512]{2,1,0:T(8,128)(2,1)} %bitcast.7), calls=%async_computation.2 | async-start | bytes 1572864 | tf_op jit(solution)/shard_map/all_to_all | solution.py:53
  120.6 0.2 all-gather.2.cloned.1.call-start
  120.9 0.1 copy.30
  121.0 13.4 %all-to-all-done.1 = bf16[16,48,512]{2,1,0:T(8,128)(2,1)S(1)} async-done(((bf16[16,48,512]{2,1,0:T(8,128)(2,1)}), bf16[16,48,512]{2,1,0:T(8,128)(2,1)S(1)}, u32[]{:S(2)}, u32[]{:S(2)}) %all-to-all-start.1) | async-done | bytes 786464 | tf_op jit(solution)/shard_map/all_to_all | solution.py:53
  134.4 2.0 gather_fusion
  136.4 0.7 reshape.161
  137.1 1.3 multiply_reduce_fusion
  138.4 1.1 fusion.6
  139.5 0.0 all-gather.2.cloned.1.call-update
  139.5 0.1 mul.102
  139.7 22.7 %all-gather.2.cloned.1.call-done = bf16[256,4096]{1,0:T(8,128)(2,1)} async-done(((bf16[256,512]{1,0:T(8,128)(2,1)}), bf16[256,4096]{1,0:T(8,128)(2,1)}) %all-gather.2.cloned.1.call-update) | async-done | bytes 2097168 | tf_op jit(solution)/shard_map/all_gather | solution.py:31
  162.4 8.2 %mul.105 = f32[256,2,4096]{2,1,0:T(2,128)} broadcast(bf16[256,4096]{1,0:T(8,128)(2,1)} %all-gather.2.cloned.1.call-done), dimensions={0,2} | broadcast | bytes 10485760 | tf_op jit(solution)/shard_map/mul | solution.py:33
  170.6 10.9 %mul.106 = f32[512,4096]{1,0:T(8,128)} reshape(f32[256,2,4096]{2,1,0:T(2,128)} %mul.105) | data formatting | bytes 16777216 | tf_op jit(solution)/shard_map/mul | solution.py:33
  181.5 12.7 %scatter_custom_fusion.1 = bf16[768,4096]{1,0:T(8,128)(2,1)} fusion(s32[512]{0:T(512)S(1)} %bitcast.63, f32[512,4096]{1,0:T(8,128)} %mul.106, f32[512]{0:T(512)S(1)} %mul.102, bf16[]{:T(256)} %constant.44.clone.1), kind=kCustom, calls=%fused_computation.7 | custom fusion | flops 4194304 | bytes 14682114 | tf_op jit(solution)/shard_map/scatter | solution.py:39
  194.2 7.0 %all-to-all-start.2 = ((bf16[16,48,4096]{2,1,0:T(8,128)(2,1)}), bf16[16,48,4096]{2,1,0:T(8,128)(2,1)}, u32[]{:S(2)}, u32[]{:S(2)}) async-start(bf16[16,48,4096]{2,1,0:T(8,128)(2,1)} %bitcast.53), calls=%async_computation.3 | async-start | bytes 12582912 | tf_op jit(solution)/shard_map/all_to_all | solution.py:44
  201.2 94.4 %all-to-all-done.2 = bf16[16,48,4096]{2,1,0:T(8,128)(2,1)} async-done(((bf16[16,48,4096]{2,1,0:T(8,128)(2,1)}), bf16[16,48,4096]{2,1,0:T(8,128)(2,1)}, u32[]{:S(2)}, u32[]{:S(2)}) %all-to-all-start.2) | async-done | bytes 6291488 | tf_op jit(solution)/shard_map/all_to_all | solution.py:44
  295.7 11.0 %convolution_convert_fusion.1 = bf16[768,1024]{1,0:T(8,128)(2,1)S(1)} fusion(bf16[768,4096]{1,0:T(8,128)(2,1)} %bitcast.11, bf16[1024,4096]{1,0:T(8,128)(2,1)} %bitcast.68), kind=kOutput, calls=%fused_computation.11 | convolution fusion | flops 6443237376 | bytes 16252928 | tf_op jit(solution)/shard_map/dot_general | solution.py:70
  306.6 1.3 convert_reduce_fusion.1
  307.9 2.4 reshape.157
  310.3 5.0 %all-to-all-start.3 = ((bf16[16,48,2,512]{3,2,1,0:T(2,128)(2,1)}), bf16[16,48,2,512]{3,2,1,0:T(2,128)(2,1)S(1)}, u32[]{:S(2)}, u32[]{:S(2)}) async-start(bf16[16,48,2,512]{3,2,1,0:T(2,128)(2,1)} %reshape.157), calls=%async_computation.4 | async-start | bytes 3145728 | tf_op jit(solution)/shard_map/all_to_all | solution.py:77
  315.3 0.6 broadcast_multiply_fusion
  315.9 11.4 %multiply_convert_fusion = bf16[1024,4096]{1,0:T(8,128)(2,1)} fusion(bf16[768,1024]{1,0:T(8,128)(2,1)} %bitcast.60, bf16[768,4096]{1,0:T(8,128)(2,1)} %bitcast.11), kind=kOutput, calls=%fused_computation.4 | convolution fusion | flops 6450839552 | bytes 16252928 | tf_op jit(solution)/shard_map/dot_general | solution.py:67
  327.2 11.3 %all-to-all-done.3 = bf16[16,48,2,512]{3,2,1,0:T(2,128)(2,1)S(1)} async-done(((bf16[16,48,2,512]{3,2,1,0:T(2,128)(2,1)}), bf16[16,48,2,512]{3,2,1,0:T(2,128)(2,1)S(1)}, u32[]{:S(2)}, u32[]{:S(2)}) %all-to-all-start.3) | async-done | bytes 1572896 | tf_op jit(solution)/shard_map/all_to_all | solution.py:77
  338.5 3.6 gather_fusion.1
  342.1 1.4 convert_reduce_fusion
  343.5 0.5 slice_add_fusion
  344.0 4.7 %scatter-add.4 = f32[256,2,512]{2,1,0:T(2,128)S(1)} dynamic-update-slice(f32[256,2,512]{2,1,0:T(2,128)S(1)} %convert_reduce_fusion, f32[256,1,512]{2,1,0:T(1,128)S(1)} %slice_add_fusion, s32[]{:T(128)} %constant.46.clone.1, s32[]{:T(128)} %constant.46.clone.1, s32[]{:T(128)} %constant.46.clone.1) | dynamic-update-slice | bytes 1048580 | tf_op jit(solution)/shard_map/scatter-add | solution.py:90
  348.8 1.2 convert_element_type.90
  (17 shorter events, 0.1 us)
Async XLA Ops:
  7.2 104.3 %reduce-scatter.2.cloned.1.call-start = ((), (), s32[]{:S(2)}) async-start(), calls=%async_computation.5 | async-start | bytes 7077888 | tf_op jit(solution)/shard_map/reduce_scatter | solution.py:49
  58.2 1.2 copy-start.1
  71.4 40.1 %copy-start.5 = (f32[1,512]{1,0:T(1,128)S(1)}, f32[1,512]{1,0:T(1,128)}, u32[]{:S(2)}) copy-start(f32[1,512]{1,0:T(1,128)} %param.13) | copy-start | bytes 6148
  71.4 49.5 %copy-start.4 = (f32[256,2]{0,1:T(2,128)S(1)}, f32[256,2]{0,1:T(2,128)}, u32[]{:S(2)}) copy-start(f32[256,2]{0,1:T(2,128)} %param.15) | copy-start | bytes 6148
  71.4 67.0 %copy-start = (bf16[256,2,512]{2,1,0:T(2,128)(2,1)S(1)}, bf16[256,2,512]{2,1,0:T(2,128)(2,1)}, u32[]{:S(2)}) copy-start(bf16[256,2,512]{2,1,0:T(2,128)(2,1)} %param.9) | copy-start | bytes 1572868
  71.4 67.0 %copy-start.2 = (bf16[256,512]{1,0:T(8,128)(2,1)S(1)}, bf16[256,512]{1,0:T(8,128)(2,1)}, u32[]{:S(2)}) copy-start(bf16[256,512]{1,0:T(8,128)(2,1)} %param.11) | copy-start | bytes 786436
  71.4 67.0 %copy-start.3 = (bf16[256,512]{1,0:T(8,128)(2,1)S(1)}, bf16[256,512]{1,0:T(8,128)(2,1)}, u32[]{:S(2)}) copy-start(bf16[256,512]{1,0:T(8,128)(2,1)} %param.10) | copy-start | bytes 786436
  113.6 20.8 %all-to-all-start.1 = ((bf16[16,48,512]{2,1,0:T(8,128)(2,1)}), bf16[16,48,512]{2,1,0:T(8,128)(2,1)S(1)}, u32[]{:S(2)}, u32[]{:S(2)}) async-start(bf16[16,48,512]{2,1,0:T(8,128)(2,1)} %bitcast.7), calls=%async_computation.2 | async-start | bytes 1572864 | tf_op jit(solution)/shard_map/all_to_all | solution.py:53
  120.6 41.8 %all-gather.2.cloned.1.call-start = ((), (), s32[]{:S(2)}) async-start(), calls=%async_computation.6 | async-start | bytes 2359296 | tf_op jit(solution)/shard_map/all_gather | solution.py:31
  194.2 101.5 %all-to-all-start.2 = ((bf16[16,48,4096]{2,1,0:T(8,128)(2,1)}), bf16[16,48,4096]{2,1,0:T(8,128)(2,1)}, u32[]{:S(2)}, u32[]{:S(2)}) async-start(bf16[16,48,4096]{2,1,0:T(8,128)(2,1)} %bitcast.53), calls=%async_computation.3 | async-start | bytes 12582912 | tf_op jit(solution)/shard_map/all_to_all | solution.py:44
  310.3 28.2 %all-to-all-start.3 = ((bf16[16,48,2,512]{3,2,1,0:T(2,128)(2,1)}), bf16[16,48,2,512]{3,2,1,0:T(2,128)(2,1)S(1)}, u32[]{:S(2)}, u32[]{:S(2)}) async-start(bf16[16,48,2,512]{3,2,1,0:T(2,128)(2,1)} %reshape.157), calls=%async_computation.4 | async-start | bytes 3145728 | tf_op jit(solution)/shard_map/all_to_all | solution.py:77
Sparse Core Ops, SparseCore 0:
  71.5 39.9 reduce-scatter.1
  139.6 22.7 all-gather.1
where the time goes:
time: 358 us; the launch traced here: 357 us
  waiting for transfers between devices  182 us (51%)
  local copies, waits for them, and re-layouts  52 us (15%)
  matrix products  34.2 us (10%)
  blocking collectives  30.7 us (9%)
  other arithmetic  24.3 us (7%)
  starting transfers between devices  19.2 us (5%)
  between operations  14.3 us (4%)
    all_to_all x1, waiting for transfers between devices, per_device(): lax.all_to_all(send_cot, 'expert', split_axis=0, concat_axis=0, tiled=True)  94.4 us
    reduce_scatter x1, waiting for transfers between devices, per_device(): lax.psum_scatter(partial_value.astype(jnp.bfloat16), 'tensor', scatter_di...  40 us
    all_to_all x1, blocking collectives, per_device(): lax.all_to_all(send_inputs, 'expert', split_axis=0, concat_axis=0, tiled=...  30.7 us
    all_gather x1, waiting for transfers between devices, per_device(): weighted_rows = lax.all_gather(weighted, 'tensor', axis=1, tiled=True)  22.7 us
    mul x3, local copies, waits for them, and re-layouts, per_device(): gate_values[:, :, None] * weighted_rows[:, None, :].astype(jnp.float32)  19.2 us
    scatter x1, local copies, waits for them, and re-layouts, per_device(): jnp.zeros((slots_total, 2, width), jnp.bfloat16).at[positions]  13.8 us
    all_to_all x1, waiting for transfers between devices, per_device(): lax.all_to_all(cross.reshape(experts, capacity, width), 'expert', split_a...  13.4 us
    scatter x1, other arithmetic, per_device(): send_cot = jnp.zeros((slots_total, cot_width), jnp.bfloat16).at[positions...  12.7 us
  transfers between devices with their start and end apart: 5, of which 5 were waited for; matrix products, arithmetic and copies ran while one was open for 3% of the time, Pallas kernels for 0%

commit v1 on v0

--- a/solution.py
+++ b/solution.py
@@ -2,6 +2,19 @@
 import jax.numpy as jnp
 from jax import lax
 from jax.sharding import PartitionSpec as P
+
+
+def gather_around(x, axis, dim):
+    ways = lax.axis_size(axis)
+    up = [(d, (d + 1) % ways) for d in range(ways)]
+    down = [(d, (d - 1) % ways) for d in range(ways)]
+    earlier, later = ([x], [x])
+    for _ in range(ways // 2):
+        earlier.append(lax.ppermute(earlier[-1], axis, up))
+    for _ in range((ways - 1) // 2):
+        later.append(lax.ppermute(later[-1], axis, down))
+    line = jnp.concatenate([*earlier[::-1], *later[1:]], axis=dim)
+    return jnp.roll(line, (lax.axis_index(axis) - ways // 2) * x.shape[dim], axis=dim)
 
 
 def route_positions(routes, experts, capacity):
@@ -28,7 +41,7 @@
     send_inputs = jnp.zeros((slots_total, 2, width), jnp.bfloat16).at[positions].set(route_inputs)
     send_inputs = send_inputs.reshape(experts, capacity, 2, width)
     weighted = (cotangent.astype(jnp.float32) * base_input.astype(jnp.float32)).astype(jnp.bfloat16)
-    weighted_rows = lax.all_gather(weighted, "tensor", axis=1, tiled=True)
+    weighted_rows = gather_around(weighted, "tensor", 1)
     cot_width = weighted_rows.shape[1]
     route_cot = (gate_values[:, :, None] * weighted_rows[:, None, :].astype(jnp.float32)).astype(
         jnp.bfloat16

time: 358 us -> 358 us (level); the launches traced: 357 us -> 352 us
  waiting for transfers between devices: 182 us -> 172 us
  starting transfers between devices: 19.2 us -> 26 us
    all_gather x1 -> x0, waiting for transfers between devices: 22.7 us -> none  [per_device(): weighted_rows = lax.all_gather(weighted, 'tensor', axis=1, tiled=True)]
    ppermute x0 -> x7, waiting for transfers between devices: none -> 19 us  [the longest x4 19 us: gather_around(): earlier.append(lax.ppermute(earlier[-1], axis, up))]
    ppermute x0 -> x7, starting transfers between devices: none -> 8.88 us  [the longest x3 8.87 us: gather_around(): later.append(lax.ppermute(later[-1], axis, down))]
    all_to_all x1, waiting for transfers between devices: 94.4 us -> 89.7 us  [per_device(): lax.all_to_all(send_cot, 'expert', split_axis=0, concat_axis=0, tiled=True)]
  transfers between devices with their start and end apart: 5 -> 11, of which waited for: 5 -> 8; matrix products, arithmetic and copies ran while one was open for 3% -> 4% of each run, Pallas kernels for 0% -> 0%
where the time goes in v1:
time: 358 us; the launch traced here: 352 us
  waiting for transfers between devices  172 us (48%)
  local copies, waits for them, and re-layouts  49.9 us (14%)
  matrix products  34.2 us (10%)
  blocking collectives  30.7 us (9%)
  starting transfers between devices  26 us (7%)
  other arithmetic  24.9 us (7%)
  between operations  14.4 us (4%)
    all_to_all x1, waiting for transfers between devices, per_device(): lax.all_to_all(send_cot, 'expert', split_axis=0, concat_axis=0, tiled=True)  89.7 us
    reduce_scatter x1, waiting for transfers between devices, per_device(): lax.psum_scatter(partial_value.astype(jnp.bfloat16), 'tensor', scatter_di...  40.1 us
    all_to_all x1, blocking collectives, per_device(): lax.all_to_all(send_inputs, 'expert', split_axis=0, concat_axis=0, tiled=...  30.7 us
    ppermute x4, waiting for transfers between devices, gather_around(): earlier.append(lax.ppermute(earlier[-1], axis, up))  19 us
    mul x3, local copies, waits for them, and re-layouts, per_device(): gate_values[:, :, None] * weighted_rows[:, None, :].astype(jnp.float32)  16.6 us
    scatter x1, local copies, waits for them, and re-layouts, per_device(): jnp.zeros((slots_total, 2, width), jnp.bfloat16).at[positions]  13.8 us
    all_to_all x1, waiting for transfers between devices, per_device(): lax.all_to_all(cross.reshape(experts, capacity, width), 'expert', split_a...  13.6 us
    scatter x1, other arithmetic, per_device(): send_cot = jnp.zeros((slots_total, cot_width), jnp.bfloat16).at[positions...  12.9 us
  transfers between devices with their start and end apart: 11, of which 8 were waited for; matrix products, arithmetic and copies ran while one was open for 4% of the time, Pallas kernels for 0%

profile of v1, /device:TPU:0, one launch (start us, length us, event | category | flops | bytes accessed | tf_op | source)
XLA Modules:
  0.0 351.8 jit_solution(1904513922638731330)
XLA Ops:
  7.2 0.7 broadcast_multiply_fusion.1
  7.9 0.8 copy.32
  8.7 0.1 eq.32
  8.9 0.1 eq.28
  9.1 0.1 mul.99
  9.3 1.2 reduce-window.6
  10.5 0.2 slice_reduce_fusion
  10.8 1.6 broadcast_in_dim.7
  12.4 0.8 broadcast_in_dim.6
  13.2 13.8 %scatter_fusion = bf16[768,2,512]{2,1,0:T(2,128)(2,1)S(1)} fusion(bf16[768,2,512]{2,1,0:T(2,128)(2,1)S(1)} %broadcast_in_dim.6, s32[512]{0:T(512)S(1)} %bitcast.61, bf16[512,2,512]{2,1,0:T(2,128)(2,1)S(1)} %bitcast.57), kind=kCustom, calls=%fused_computation.2 | custom fusion | bytes 3147776 | tf_op jit(solution)/shard_map/scatter | solution.py:41
  27.1 30.7 %all_to_all.20 = bf16[16,48,2,512]{3,2,1,0:T(2,128)(2,1)S(1)} all-to-all(bf16[16,48,2,512]{3,2,1,0:T(2,128)(2,1)S(1)} %bitcast.54), channel_id=1, replica_groups=mesh['expert'=16,'tensor'=8] {'expert'}, dimensions={0} | all-to-all | bytes 3145728 | tf_op jit(solution)/shard_map/all_to_all | solution.py:56
  57.8 0.4 copy.39
  58.2 1.2 copy-done.1
  59.5 11.9 %convolution_convert_fusion = bf16[768,4096]{1,0:T(8,128)(2,1)} fusion(bf16[768,1024]{1,0:T(8,128)(2,1)S(1)} %bitcast.59, bf16[1024,4096]{1,0:T(8,128)(2,1)} %bitcast.67), kind=kOutput, calls=%fused_computation.6 | convolution fusion | flops 6445596672 | bytes 16252928 | tf_op jit(solution)/shard_map/dot_general | solution.py:61
  71.4 40.1 %reduce-scatter.2.cloned.1.call-done = bf16[768,512]{1,0:T(8,128)(2,1)} async-done(((bf16[768,4096]{1,0:T(8,128)(2,1)}), bf16[768,512]{1,0:T(8,128)(2,1)}) %reduce-scatter.2.cloned.1.call-update) | async-done | bytes 786448 | tf_op jit(solution)/shard_map/reduce_scatter | solution.py:62
  111.5 2.2 add_convert_fusion
  113.6 7.0 %all-to-all-start.1 = ((bf16[16,48,512]{2,1,0:T(8,128)(2,1)}), bf16[16,48,512]{2,1,0:T(8,128)(2,1)S(1)}, u32[]{:S(2)}, u32[]{:S(2)}) async-start(bf16[16,48,512]{2,1,0:T(8,128)(2,1)} %bitcast.7), calls=%async_computation.2 | async-start | bytes 1572864 | tf_op jit(solution)/shard_map/all_to_all | solution.py:66
  120.8 13.6 %all-to-all-done.1 = bf16[16,48,512]{2,1,0:T(8,128)(2,1)S(1)} async-done(((bf16[16,48,512]{2,1,0:T(8,128)(2,1)}), bf16[16,48,512]{2,1,0:T(8,128)(2,1)S(1)}, u32[]{:S(2)}, u32[]{:S(2)}) %all-to-all-start.1) | async-done | bytes 786464 | tf_op jit(solution)/shard_map/all_to_all | solution.py:66
  134.4 2.0 gather_fusion
  136.4 0.7 reshape.161
  137.1 1.3 multiply_reduce_fusion
  138.4 1.0 fusion.6
  139.4 7.0 %collective-permute-done = bf16[256,512]{1,0:T(8,128)(2,1)S(1)} collective-permute-done((bf16[256,512]{1,0:T(8,128)(2,1)S(1)}, bf16[256,512]{1,0:T(8,128)(2,1)S(1)}, u32[]{:S(2)}, u32[]{:S(2)}) %collective-permute-start) | collective-permute-done | bytes 262176 | tf_op jit(solution)/shard_map/ppermute | solution.py:13
  146.4 3.0 collective-permute-start.4
  149.4 4.1 %collective-permute-done.1 = bf16[256,512]{1,0:T(8,128)(2,1)S(1)} collective-permute-done((bf16[256,512]{1,0:T(8,128)(2,1)S(1)}, bf16[256,512]{1,0:T(8,128)(2,1)S(1)}, u32[]{:S(2)}, u32[]{:S(2)}) %collective-permute-start.1) | collective-permute-done | bytes 262176 | tf_op jit(solution)/shard_map/ppermute | solution.py:13
  153.5 3.0 collective-permute-start.5
  156.4 4.0 %collective-permute-done.2 = bf16[256,512]{1,0:T(8,128)(2,1)S(1)} collective-permute-done((bf16[256,512]{1,0:T(8,128)(2,1)S(1)}, bf16[256,512]{1,0:T(8,128)(2,1)S(1)}, u32[]{:S(2)}, u32[]{:S(2)}) %collective-permute-start.2) | collective-permute-done | bytes 262176 | tf_op jit(solution)/shard_map/ppermute | solution.py:13
  160.5 0.1 mul.105
  160.6 3.0 collective-permute-start.6
  163.6 3.9 %collective-permute-done.3 = bf16[256,512]{1,0:T(8,128)(2,1)S(1)} collective-permute-done((bf16[256,512]{1,0:T(8,128)(2,1)S(1)}, bf16[256,512]{1,0:T(8,128)(2,1)S(1)}, u32[]{:S(2)}, u32[]{:S(2)}) %collective-permute-start.3) | collective-permute-done | bytes 262176 | tf_op jit(solution)/shard_map/ppermute | solution.py:13
  168.0 0.5 dynamic-slice_convert_fusion
  168.5 5.6 %mul.109 = f32[256,2,4096]{2,1,0:T(2,128)} broadcast(f32[256,4096]{1,0:T(8,128)S(1)} %dynamic-slice_convert_fusion), dimensions={0,2} | broadcast | bytes 12582912 | tf_op jit(solution)/shard_map/mul | solution.py:46
  174.2 10.9 %mul.110 = f32[512,4096]{1,0:T(8,128)} reshape(f32[256,2,4096]{2,1,0:T(2,128)} %mul.109) | data formatting | bytes 16777216 | tf_op jit(solution)/shard_map/mul | solution.py:46
  185.0 12.9 %scatter_custom_fusion.1 = bf16[768,4096]{1,0:T(8,128)(2,1)} fusion(s32[512]{0:T(512)S(1)} %bitcast.63, f32[512,4096]{1,0:T(8,128)} %mul.110, f32[512]{0:T(512)S(1)} %mul.105, bf16[]{:T(256)} %constant.64.clone.1), kind=kCustom, calls=%fused_computation.7 | custom fusion | flops 4194304 | bytes 14682114 | tf_op jit(solution)/shard_map/scatter | solution.py:52
  198.0 4.6 %all-to-all-start.2 = ((bf16[16,48,4096]{2,1,0:T(8,128)(2,1)}), bf16[16,48,4096]{2,1,0:T(8,128)(2,1)}, u32[]{:S(2)}, u32[]{:S(2)}) async-start(bf16[16,48,4096]{2,1,0:T(8,128)(2,1)} %bitcast.53), calls=%async_computation.3 | async-start | bytes 12582912 | tf_op jit(solution)/shard_map/all_to_all | solution.py:57
  202.6 89.7 %all-to-all-done.2 = bf16[16,48,4096]{2,1,0:T(8,128)(2,1)} async-done(((bf16[16,48,4096]{2,1,0:T(8,128)(2,1)}), bf16[16,48,4096]{2,1,0:T(8,128)(2,1)}, u32[]{:S(2)}, u32[]{:S(2)}) %all-to-all-start.2) | async-done | bytes 6291488 | tf_op jit(solution)/shard_map/all_to_all | solution.py:57
  292.3 11.0 %convolution_convert_fusion.1 = bf16[768,1024]{1,0:T(8,128)(2,1)S(1)} fusion(bf16[768,4096]{1,0:T(8,128)(2,1)} %bitcast.11, bf16[1024,4096]{1,0:T(8,128)(2,1)} %bitcast.68), kind=kOutput, calls=%fused_computation.12 | convolution fusion | flops 6443237376 | bytes 16252928 | tf_op jit(solution)/shard_map/dot_general | solution.py:83
  303.3 1.3 convert_reduce_fusion.1
  304.6 2.4 reshape.157
  307.0 5.4 %all-to-all-start.3 = ((bf16[16,48,2,512]{3,2,1,0:T(2,128)(2,1)}), bf16[16,48,2,512]{3,2,1,0:T(2,128)(2,1)S(1)}, u32[]{:S(2)}, u32[]{:S(2)}) async-start(bf16[16,48,2,512]{3,2,1,0:T(2,128)(2,1)} %reshape.157), calls=%async_computation.4 | async-start | bytes 3145728 | tf_op jit(solution)/shard_map/all_to_all | solution.py:90
  312.4 0.6 broadcast_multiply_fusion
  313.0 11.4 %multiply_convert_fusion = bf16[1024,4096]{1,0:T(8,128)(2,1)} fusion(bf16[768,1024]{1,0:T(8,128)(2,1)} %bitcast.60, bf16[768,4096]{1,0:T(8,128)(2,1)} %bitcast.11), kind=kOutput, calls=%fused_computation.4 | convolution fusion | flops 6450839552 | bytes 16252928 | tf_op jit(solution)/shard_map/dot_general | solution.py:80
  324.3 9.2 %all-to-all-done.3 = bf16[16,48,2,512]{3,2,1,0:T(2,128)(2,1)S(1)} async-done(((bf16[16,48,2,512]{3,2,1,0:T(2,128)(2,1)}), bf16[16,48,2,512]{3,2,1,0:T(2,128)(2,1)S(1)}, u32[]{:S(2)}, u32[]{:S(2)}) %all-to-all-start.3) | async-done | bytes 1572896 | tf_op jit(solution)/shard_map/all_to_all | solution.py:90
  333.5 3.6 %gather_fusion.1 = bf16[512,2,512]{2,1,0:T(2,128)(2,1)S(1)} fusion(bf16[768,2,512]{2,1,0:T(2,128)(2,1)S(1)} %bitcast.56, s32[1024]{0:T(1024)S(1)} %pad_clamp_fusion), kind=kCustom, calls=%fused_computation.1 | custom fusion | bytes 2099200 | tf_op jit(solution)/shard_map/gather | solution.py:98
  337.1 1.4 convert_reduce_fusion
  338.6 0.5 slice_add_fusion
  339.1 4.7 %scatter-add.4 = f32[256,2,512]{2,1,0:T(2,128)S(1)} dynamic-update-slice(f32[256,2,512]{2,1,0:T(2,128)S(1)} %convert_reduce_fusion, f32[256,1,512]{2,1,0:T(1,128)S(1)} %slice_add_fusion, s32[]{:T(128)} %constant.66.clone.1, s32[]{:T(128)} %constant.66.clone.1, s32[]{:T(128)} %constant.66.clone.1) | dynamic-update-slice | bytes 1048580 | tf_op jit(solution)/shard_map/scatter-add | solution.py:103
  343.8 1.2 convert_element_type.90
  (45 shorter events, 1.0 us)
Async XLA Ops:
  7.2 104.3 %reduce-scatter.2.cloned.1.call-start = ((), (), s32[]{:S(2)}) async-start(), calls=%async_computation.5 | async-start | bytes 7077888 | tf_op jit(solution)/shard_map/reduce_scatter | solution.py:62
  58.2 1.2 copy-start.1
  71.4 40.1 %copy-start.5 = (f32[1,512]{1,0:T(1,128)S(1)}, f32[1,512]{1,0:T(1,128)}, u32[]{:S(2)}) copy-start(f32[1,512]{1,0:T(1,128)} %param.13) | copy-start | bytes 6148
  71.4 49.3 %copy-start.4 = (f32[256,2]{0,1:T(2,128)S(1)}, f32[256,2]{0,1:T(2,128)}, u32[]{:S(2)}) copy-start(f32[256,2]{0,1:T(2,128)} %param.15) | copy-start | bytes 6148
  113.6 20.8 %all-to-all-start.1 = ((bf16[16,48,512]{2,1,0:T(8,128)(2,1)}), bf16[16,48,512]{2,1,0:T(8,128)(2,1)S(1)}, u32[]{:S(2)}, u32[]{:S(2)}) async-start(bf16[16,48,512]{2,1,0:T(8,128)(2,1)} %bitcast.7), calls=%async_computation.2 | async-start | bytes 1572864 | tf_op jit(solution)/shard_map/all_to_all | solution.py:66
  120.6 17.8 %copy-start = (bf16[256,2,512]{2,1,0:T(2,128)(2,1)S(1)}, bf16[256,2,512]{2,1,0:T(2,128)(2,1)}, u32[]{:S(2)}) copy-start(bf16[256,2,512]{2,1,0:T(2,128)(2,1)} %param.9) | copy-start | bytes 1572868
  120.6 17.8 %copy-start.2 = (bf16[256,512]{1,0:T(8,128)(2,1)S(1)}, bf16[256,512]{1,0:T(8,128)(2,1)}, u32[]{:S(2)}) copy-start(bf16[256,512]{1,0:T(8,128)(2,1)} %param.11) | copy-start | bytes 786436
  120.7 17.8 %copy-start.3 = (bf16[256,512]{1,0:T(8,128)(2,1)S(1)}, bf16[256,512]{1,0:T(8,128)(2,1)}, u32[]{:S(2)}) copy-start(bf16[256,512]{1,0:T(8,128)(2,1)} %param.10) | copy-start | bytes 786436
  139.4 7.0 %collective-permute-start = (bf16[256,512]{1,0:T(8,128)(2,1)S(1)}, bf16[256,512]{1,0:T(8,128)(2,1)S(1)}, u32[]{:S(2)}, u32[]{:S(2)}) collective-permute-start(bf16[256,512]{1,0:T(8,128)(2,1)S(1)} %get-tuple-element.29), channel_id=1, source_target_pairs={{0,1},{1,2},{2,3},{3,4},{4,5},{5,6},{6,7},{7,0},{8,9},{9,10},{10,1... | collective-permute-start | bytes 786440 | tf_op jit(solution)/shard_map/ppermute | solution.py:13
  146.4 7.0 %collective-permute-start.1 = (bf16[256,512]{1,0:T(8,128)(2,1)S(1)}, bf16[256,512]{1,0:T(8,128)(2,1)S(1)}, u32[]{:S(2)}, u32[]{:S(2)}) collective-permute-start(bf16[256,512]{1,0:T(8,128)(2,1)S(1)} %collective-permute-done), channel_id=1, source_target_pairs={{0,1},{1,2},{2,3},{3,4},{4,5},{5,6},{6,7},{7,0},{8,9},{9,10},{10,1... | collective-permute-start | bytes 786440 | tf_op jit(solution)/shard_map/ppermute | solution.py:13
  146.4 7.0 %collective-permute-start.4 = (bf16[256,512]{1,0:T(8,128)(2,1)S(1)}, bf16[256,512]{1,0:T(8,128)(2,1)S(1)}, u32[]{:S(2)}, u32[]{:S(2)}) collective-permute-start(bf16[256,512]{1,0:T(8,128)(2,1)S(1)} %get-tuple-element.29), channel_id=1, source_target_pairs={{0,7},{1,0},{2,1},{3,2},{4,3},{5,4},{6,5},{7,6},{8,15},{9,8},{10,9... | collective-permute-start | bytes 786440 | tf_op jit(solution)/shard_map/ppermute | solution.py:15
  153.5 7.0 %collective-permute-start.2 = (bf16[256,512]{1,0:T(8,128)(2,1)S(1)}, bf16[256,512]{1,0:T(8,128)(2,1)S(1)}, u32[]{:S(2)}, u32[]{:S(2)}) collective-permute-start(bf16[256,512]{1,0:T(8,128)(2,1)S(1)} %collective-permute-done.1), channel_id=1, source_target_pairs={{0,1},{1,2},{2,3},{3,4},{4,5},{5,6},{6,7},{7,0},{8,9},{9,10},{10,1... | collective-permute-start | bytes 786440 | tf_op jit(solution)/shard_map/ppermute | solution.py:13
  153.5 7.2 %collective-permute-start.5 = (bf16[256,512]{1,0:T(8,128)(2,1)S(1)}, bf16[256,512]{1,0:T(8,128)(2,1)S(1)}, u32[]{:S(2)}, u32[]{:S(2)}) collective-permute-start(bf16[256,512]{1,0:T(8,128)(2,1)S(1)} %collective-permute-done.4), channel_id=1, source_target_pairs={{0,7},{1,0},{2,1},{3,2},{4,3},{5,4},{6,5},{7,6},{8,15},{9,8},{10,9... | collective-permute-start | bytes 786440 | tf_op jit(solution)/shard_map/ppermute | solution.py:15
  160.5 7.0 %collective-permute-start.3 = (bf16[256,512]{1,0:T(8,128)(2,1)S(1)}, bf16[256,512]{1,0:T(8,128)(2,1)S(1)}, u32[]{:S(2)}, u32[]{:S(2)}) collective-permute-start(bf16[256,512]{1,0:T(8,128)(2,1)S(1)} %collective-permute-done.2), channel_id=1, source_target_pairs={{0,1},{1,2},{2,3},{3,4},{4,5},{5,6},{6,7},{7,0},{8,9},{9,10},{10,1... | collective-permute-start | bytes 786440 | tf_op jit(solution)/shard_map/ppermute | solution.py:13
  160.6 7.1 %collective-permute-start.6 = (bf16[256,512]{1,0:T(8,128)(2,1)S(1)}, bf16[256,512]{1,0:T(8,128)(2,1)S(1)}, u32[]{:S(2)}, u32[]{:S(2)}) collective-permute-start(bf16[256,512]{1,0:T(8,128)(2,1)S(1)} %collective-permute-done.5), channel_id=1, source_target_pairs={{0,7},{1,0},{2,1},{3,2},{4,3},{5,4},{6,5},{7,6},{8,15},{9,8},{10,9... | collective-permute-start | bytes 786440 | tf_op jit(solution)/shard_map/ppermute | solution.py:15
  198.0 94.3 %all-to-all-start.2 = ((bf16[16,48,4096]{2,1,0:T(8,128)(2,1)}), bf16[16,48,4096]{2,1,0:T(8,128)(2,1)}, u32[]{:S(2)}, u32[]{:S(2)}) async-start(bf16[16,48,4096]{2,1,0:T(8,128)(2,1)} %bitcast.53), calls=%async_computation.3 | async-start | bytes 12582912 | tf_op jit(solution)/shard_map/all_to_all | solution.py:57
  307.0 26.6 %all-to-all-start.3 = ((bf16[16,48,2,512]{3,2,1,0:T(2,128)(2,1)}), bf16[16,48,2,512]{3,2,1,0:T(2,128)(2,1)S(1)}, u32[]{:S(2)}, u32[]{:S(2)}) async-start(bf16[16,48,2,512]{3,2,1,0:T(2,128)(2,1)} %reshape.157), calls=%async_computation.4 | async-start | bytes 3145728 | tf_op jit(solution)/shard_map/all_to_all | solution.py:90
Sparse Core Ops, SparseCore 0:
  71.5 39.9 reduce-scatter.1
